TPU v7x, 32 devices: a whole 2x2x4 slice. The times are simulated.
32 devices in a mesh: dp: 8 (over z, core), sp: 4 (over y, x).
Axes of the slice: x: 2, y: 2, z: 4, core: 2. Of those that a mesh axis runs over, the one named last changes fastest.
Arguments:
- gate_pre: bfloat16 [2048, 8192], P('dp', 'sp'), may hold values from -6 to 6
- up_pre: bfloat16 [2048, 8192], P('dp', 'sp'), may hold values from -6 to 6
- w_down: bfloat16 [8192, 6144], P('sp'), may hold values from -0.0625 to 0.0625
- route_logits: float32 [4096, 2], P(('dp', 'sp')), may hold values from -8 to 8
- expert_ids: int32 [4096, 2], P(('dp', 'sp')), may hold values from 0 to 7, as said below
- d_out: bfloat16 [4096, 6144], P(('dp', 'sp')), may hold values from -6 to 6
Outputs:
- mixed: bfloat16 [4096, 6144], P(('dp', 'sp'))
- logit_grads: float32 [4096, 2], P(('dp', 'sp'))
- gate_grads: bfloat16 [2048, 8192], P('dp', 'sp')
- up_grads: bfloat16 [2048, 8192], P('dp', 'sp')
- down_grads: float32 [8192, 6144], P('sp', 'dp')
Inputs may be any that keep to these rules, and one draw needn't show every extreme that they name: `expert_ids`: each row names two different experts. Of the 128 rows of one device, a quarter of 64 up to 64 name expert 0, and exactly 64 on some device in every draw.
All inputs are finite; a program needn't handle non-finite values.
Results may differ from a plain program's by a relative error of at most 0.022.
Values may be sent and summed in bfloat16 or wider, within the bound.
A program may use at most 128 MiB of HBM per device.

v0:
```python
import functools

import jax
import jax.numpy as jnp
from jax import lax
from jax.experimental import pallas as pl
from jax.experimental.pallas import tpu as pltpu
from jax.sharding import PartitionSpec as P

MESH = pl.DeviceIdType.MESH


def exchange_kernel(
    n_dp, n_sp, hid_ref, slot_choose_ref, slot_weight_ref, w_ref, choose_ref, weight_ref, dout_ref,
    dhid_ref, hall_ref, dall_ref, mixed_ref, wgrad_ref,
    dslot_ref, part, rs_ref, dcyc, wcol, wrow, wsem, local_sem,
    right_send, left_send, pair_send, hrecv, asend, arecv, gsend, grecv, bsend, brecv, rsend, rrecv, fsend, frecv,
):
    dp, sp = lax.axis_index("dp"), lax.axis_index("sp")
    chips = n_dp // 2
    chip, core = lax.div(dp, 2), lax.rem(dp, 2)
    slot_rows, width = dslot_ref.shape
    block = width // n_dp
    hid_width = hid_ref.shape[1]
    tn = wcol.shape[2]
    th = wrow.shape[1]
    n_col, n_row = width // tn, hid_width // th

    barrier = pltpu.get_barrier_semaphore()
    for off in range(1, n_dp):
        pl.semaphore_signal(barrier, inc=1, device_id={"dp": lax.rem(dp + off, n_dp)}, device_id_type=MESH)
    for off in range(1, n_sp):
        pl.semaphore_signal(barrier, inc=1, device_id={"sp": lax.rem(sp + off, n_sp)}, device_id_type=MESH)

    def col_load(step, slot):
        return pltpu.make_async_copy(
            w_ref.at[:, pl.ds(pl.multiple_of(step * tn, tn), tn)], wcol.at[slot], wsem.at[slot]
        )

    def row_load(step, slot):
        return pltpu.make_async_copy(
            w_ref.at[pl.ds(pl.multiple_of(step * th, th), th), :], wrow.at[slot], wsem.at[2 + slot]
        )

    col_load(0, 0).start()
    row_load(0, 0).start()
    pl.semaphore_wait(barrier, n_dp - 1 + n_sp - 1)

    def remote(src, dst, send, recv, **where):
        return pltpu.make_async_remote_copy(
            src_ref=src, dst_ref=dst, send_sem=send, recv_sem=recv, device_id=where, device_id_type=MESH
        )

    def a_send(off):
        other = lax.rem(dp + off, n_dp)
        return remote(
            dslot_ref.at[:, pl.ds(pl.multiple_of(other * block, block), block)], dall_ref.at[dp, sp],
            asend.at[off], arecv.at[dp], dp=other,
        )

    def a_wait(off):
        other = lax.rem(dp + off, n_dp)
        pltpu.make_async_copy(dall_ref.at[other, sp], dall_ref.at[other, sp], arecv.at[other]).wait()

    half_slots = hid_ref.shape[0] // 2

    def h_part(index, half):
        return hall_ref.at[index, half * half_slots:(half + 1) * half_slots]

    def own_part(half):
        return hid_ref.at[half * half_slots:(half + 1) * half_slots]

    def h_send(index, half, src, to, send):
        return remote(src, h_part(index, half), send, hrecv.at[2 * index + half], dp=to)

    def h_wait(index, half):
        pltpu.make_async_copy(h_part(index, half), h_part(index, half), hrecv.at[2 * index + half]).wait()

    def h_right(index, half, src, step):
        return h_send(index, half, src, dp + 2, right_send.at[2 * step + half])

    def h_left(index, half, src, step):
        return h_send(index, half, src, dp - 2, left_send.at[2 * step + half])

    def h_pair(index, half, src):
        return h_send(index, half, src, chip * 2 + 1 - core, pair_send.at[2 * lax.div(index, 2) + half])

    for half in range(2):
        @pl.when(chip + 1 < chips)
        def _():
            h_right(dp, half, own_part(half), 0).start()

        @pl.when(chip >= 1)
        def _():
            h_left(dp, half, own_part(half), 0).start()

    for half in range(2):
        h_pair(dp, half, own_part(half)).start()

    def slot_step(step, carry):
        cols = pl.ds(pl.multiple_of(step * tn, tn), tn)
        picked = jnp.dot(slot_choose_ref[...], dout_ref[:, cols], preferred_element_type=jnp.float32)
        dslot_ref[:, cols] = (slot_weight_ref[...] * picked).astype(jnp.bfloat16)
        return carry

    lax.fori_loop(0, n_col, slot_step, 0)

    for off in range(1, n_dp):
        a_send(off).start()

    relayed = n_sp == 4
    if relayed:
        near = [sp + 1 - 2 * lax.rem(sp, 2), lax.rem(sp + 2, 4)]
    else:
        near = [lax.rem(sp + off, n_sp) for off in range(1, n_sp)]
    half_rows, half_dp = slot_rows // 2, n_dp // 2

    def g_send(way):
        return remote(dslot_ref, dcyc.at[sp], gsend.at[way], grecv.at[sp], sp=near[way])

    def b_send(way):
        return remote(dall_ref.at[:, sp], dall_ref.at[:, sp], bsend.at[way], brecv.at[sp], sp=near[way])

    def g_half(source, way):
        return dcyc.at[source, way * half_rows:(way + 1) * half_rows]

    def b_half(source, way):
        return dall_ref.at[way * half_dp:(way + 1) * half_dp, source]

    def g_pass(way):
        held = g_half(near[way], way)
        return remote(held, held, fsend.at[way], frecv.at[way], sp=near[1 - way])

    def b_pass(way):
        held = b_half(near[way], way)
        return remote(held, held, fsend.at[2 + way], frecv.at[2 + way], sp=near[1 - way])

    def arrived(ref, sem):
        pltpu.make_async_copy(ref, ref, sem).wait()

    ways = range(len(near))
    for way in ways:
        g_send(way).start()

    own = [
        pltpu.make_async_copy(dslot_ref, dcyc.at[sp], local_sem.at[0]),
        pltpu.make_async_copy(
            dslot_ref.at[:, pl.ds(pl.multiple_of(dp * block, block), block)], dall_ref.at[dp, sp], local_sem.at[1]
        ),
        pltpu.make_async_copy(hid_ref, hall_ref.at[dp], local_sem.at[2]),
    ]
    for copy in own:
        copy.start()

    def r_send(step, off):
        other = lax.rem(sp + off, n_sp)
        cols = pl.ds(pl.multiple_of(step * tn, tn), tn)
        return remote(
            part.at[other, :, cols], rs_ref.at[sp, :, cols],
            rsend.at[step, off], rrecv.at[step, sp], sp=other,
        )

    def half_cols(step, way):
        half = tn // 2
        return pl.ds(pl.multiple_of(step * tn + way * half, half), half)

    def r_hop(step, way, kind):
        cols = half_cols(step, way)
        src = [part.at[near[way], :, cols], part.at[3 - sp, :, cols], rs_ref.at[3, :, cols]][kind]
        return remote(
            src, rs_ref.at[kind, :, cols], rsend.at[step, 2 * kind + way], rrecv.at[step, 2 * kind + way],
            sp=near[1 - way if kind == 2 else way],
        )

    def r_arrived(step, way, kind):
        arrived(rs_ref.at[kind, :, half_cols(step, way)], rrecv.at[step, 2 * kind + way])

    def fold_step(step, carry):
        for way in range(2):
            cols = half_cols(step, way)
            r_arrived(step, way, 1)
            rs_ref[3, :, cols] = (
                part[near[1 - way], :, cols].astype(jnp.float32) + rs_ref[1, :, cols].astype(jnp.float32)
            ).astype(jnp.bfloat16)
            r_hop(step, way, 2).start()
        return carry

    def col_step(step, carry):
        slot = lax.rem(step, 2)

        @pl.when(step + 1 < n_col)
        def _():
            col_load(step + 1, 1 - slot).start()

        col_load(step, slot).wait()
        cols = pl.ds(pl.multiple_of(step * tn, tn), tn)
        product = jnp.dot(hid_ref[...], wcol[slot], preferred_element_type=jnp.float32)
        part[:, :, cols] = product.astype(jnp.bfloat16).reshape(n_sp, slot_rows, tn)
        if relayed:
            for kind in (1, 0):
                for way in range(2):
                    r_hop(step, way, kind).start()
        else:
            for off in range(1, n_sp):
                r_send(step, off).start()
        return carry

    lax.fori_loop(0, n_col, col_step, 0)

    def relay(step, half):
        @pl.when(chip - step >= 0)
        def _():
            index = dp - 2 * step
            h_wait(index, half)

            @pl.when(chip + 1 < chips)
            def _():
                h_right(index, half, h_part(index, half), step).start()

            h_pair(index, half, h_part(index, half)).start()

        @pl.when(chip + step < chips)
        def _():
            index = dp + 2 * step
            h_wait(index, half)

            @pl.when(chip >= 1)
            def _():
                h_left(index, half, h_part(index, half), step).start()

            h_pair(index, half, h_part(index, half)).start()

    for way in ways:
        arrived(dcyc.at[near[way]], grecv.at[near[way]])
        if relayed:
            g_pass(way).start()

    if chips > 1:
        for half in range(2):
            relay(1, half)

    if relayed:
        lax.fori_loop(0, n_col, fold_step, 0)

    for copy in own:
        copy.wait()
    for off in range(1, n_dp):
        a_wait(off)

    for way in ways:
        b_send(way).start()

    if relayed:
        for way in ways:
            arrived(g_half(3 - sp, way), frecv.at[way])

    def row_step(step, carry):
        slot = lax.rem(step, 2)

        @pl.when(step + 1 < n_row)
        def _():
            row_load(step + 1, 1 - slot).start()

        row_load(step, slot).wait()
        dhid_ref[:, pl.ds(pl.multiple_of(step * th, th), th)] = lax.dot_general(
            dcyc[...].reshape(n_sp * slot_rows, width), wrow[slot], (((1,), (1,)), ((), ())),
            preferred_element_type=jnp.float32,
        )
        return carry

    for half in range(2):
        lax.fori_loop(half * n_row // 2, (half + 1) * n_row // 2, row_step, 0)
        if chips > 2:
            relay(2, half)

    wgrad_ref[...] = jnp.zeros_like(wgrad_ref)

    def mix_step(step, carry):
        cols = pl.ds(pl.multiple_of(step * tn, tn), tn)
        total = part[sp, :, cols].astype(jnp.float32)
        if relayed:
            for kind in (0, 2):
                for way in range(2):
                    r_arrived(step, way, kind)
                total = total + rs_ref[kind, :, cols].astype(jnp.float32)
        else:
            for off in range(1, n_sp):
                other = lax.rem(sp + off, n_sp)
                arrived(rs_ref.at[other, :, cols], rrecv.at[step, other])
                total = total + rs_ref[other, :, cols].astype(jnp.float32)
        high = total.astype(jnp.bfloat16)
        low = (total - high.astype(jnp.float32)).astype(jnp.bfloat16)
        token_out = jnp.dot(choose_ref[...], high, preferred_element_type=jnp.float32) + jnp.dot(
            choose_ref[...], low, preferred_element_type=jnp.float32
        )
        mixed_ref[:, cols] = (weight_ref[...] * token_out).astype(jnp.bfloat16)
        wgrad_ref[...] += jnp.sum(dout_ref[:, cols].astype(jnp.float32) * token_out, axis=1, keepdims=True)
        if relayed:
            for kind in range(3):
                for way in range(2):
                    r_hop(step, way, kind).wait_send()
        else:
            for off in range(1, n_sp):
                r_send(step, off).wait_send()
        return carry

    lax.fori_loop(0, n_col, mix_step, 0)

    for way in ways:
        arrived(dall_ref.at[:, near[way]], brecv.at[near[way]])
        if relayed:
            b_pass(way).start()

    for step in range(3, chips):
        for half in range(2):
            relay(step, half)

    for index in range(chips):
        for half in range(2):
            h_wait(index * 2 + 1 - core, half)
    for way in ways:
        g_send(way).wait_send()
        b_send(way).wait_send()
        if relayed:
            arrived(b_half(3 - sp, way), frecv.at[2 + way])
            g_pass(way).wait_send()
            b_pass(way).wait_send()
    for off in range(1, n_dp):
        a_send(off).wait_send()
    for step in range(chips):
        for half in range(2):
            @pl.when((chip - step >= 0) & (chip + 1 < chips))
            def _():
                h_right(dp - 2 * step, half, own_part(half), step).wait_send()

            @pl.when((chip + step < chips) & (chip >= 1))
            def _():
                h_left(dp + 2 * step, half, own_part(half), step).wait_send()

            h_send(dp, half, own_part(half), chip * 2 + 1 - core, pair_send.at[2 * step + half]).wait_send()


def exchange(n_dp, n_sp, hidden, slot_choose, slot_weight, w_down, choose, weight, d_out):
    slots, hid_width = hidden.shape
    slot_rows, width = slot_choose.shape[0], d_out.shape[1]
    block = width // n_dp
    tn, th = width // 8, min(256, hid_width)
    n_col = width // tn
    chips = n_dp // 2
    bf = jnp.bfloat16
    dma = pltpu.SemaphoreType.DMA
    hbm = pl.BlockSpec(memory_space=pl.ANY)
    vmem = pl.BlockSpec(memory_space=pltpu.VMEM)
    return pl.pallas_call(
        functools.partial(exchange_kernel, n_dp, n_sp),
        out_shape=(
            jax.ShapeDtypeStruct((slots, hid_width), jnp.float32),
            jax.ShapeDtypeStruct((n_dp, slots, hid_width), bf),
            jax.ShapeDtypeStruct((n_dp, n_sp, slot_rows, block), bf),
            jax.ShapeDtypeStruct(d_out.shape, bf),
            jax.ShapeDtypeStruct((d_out.shape[0], 1), jnp.float32),
        ),
        in_specs=[vmem, vmem, vmem, hbm, vmem, vmem, vmem],
        out_specs=(vmem, hbm, hbm, vmem, vmem),
        scratch_shapes=[
            pltpu.VMEM((slot_rows, width), bf),
            pltpu.VMEM((n_sp, slot_rows, width), bf),
            pltpu.VMEM((n_sp, slot_rows, width), bf),
            pltpu.VMEM((n_sp, slot_rows, width), bf),
            pltpu.VMEM((2, hid_width, tn), bf),
            pltpu.VMEM((2, th, width), bf),
            dma((4,)),
            dma((4,)),
            dma((2 * chips,)),
            dma((2 * chips,)),
            dma((2 * chips,)),
            dma((2 * n_dp,)),
            dma((n_dp,)),
            dma((n_dp,)),
            dma((n_sp,)),
            dma((n_sp,)),
            dma((n_sp,)),
            dma((n_sp,)),
            dma((n_col, max(n_sp, 6))),
            dma((n_col, max(n_sp, 6))),
            dma((4,)),
            dma((4,)),
        ],
        compiler_params=pltpu.CompilerParams(
            collective_id=0, has_side_effects=True, vmem_limit_bytes=60 * 1024 * 1024
        ),
    )(hidden, slot_choose, slot_weight, w_down, choose, weight, d_out)


def contract_rows(left, right):
    return lax.dot_general(
        left, right, (((0,), (0,)), ((), ())), preferred_element_type=jnp.float32
    )


def local(n_dp, n_sp, gate_pre, up_pre, w_down, route_logits, expert_ids, d_out):
    tok_rows = expert_ids.shape[0]
    slot_rows = tok_rows // 2
    routed = jnp.any(expert_ids == 0, axis=1)
    routed_int = routed.astype(jnp.int32)
    routed_float = routed.astype(jnp.float32)
    slot_rank = jnp.cumsum(routed_int) - 1
    gate_wide = gate_pre.astype(jnp.float32)
    up_wide = up_pre.astype(jnp.float32)
    sigma_gate = jax.nn.sigmoid(gate_wide)
    silu_gate = gate_wide * sigma_gate
    hidden = (silu_gate * up_wide).astype(jnp.bfloat16)
    first_zero = expert_ids[:, 0] == 0
    own_logit = jnp.where(first_zero, route_logits[:, 0], route_logits[:, 1])
    other_logit = jnp.where(first_zero, route_logits[:, 1], route_logits[:, 0])
    weight_zero = routed_float * jax.nn.sigmoid(own_logit - other_logit)
    chooser = (slot_rank[:, None] == jnp.arange(slot_rows, dtype=jnp.int32)[None, :]) & routed[
        :, None
    ]
    slot_weight = jnp.sum(jnp.where(chooser, weight_zero[:, None], 0.0), axis=0)
    d_hidden, hidden_all, d_all, mixed, weight_grad = exchange(
        n_dp, n_sp, hidden, chooser.T.astype(jnp.bfloat16), slot_weight[:, None], w_down, chooser.astype(jnp.bfloat16), weight_zero[:, None], d_out
    )
    logit_grad = weight_grad[:, 0] * weight_zero * (1.0 - weight_zero)
    first_col = jnp.where(first_zero, logit_grad, -logit_grad)
    logit_grads = jnp.stack([first_col, -first_col], axis=1)
    down_grads = contract_rows(
        hidden_all.reshape(-1, hidden_all.shape[-1]), d_all.reshape(-1, d_all.shape[-1])
    )
    gate_grads = (d_hidden * up_wide * sigma_gate * (1.0 + gate_wide * (1.0 - sigma_gate))).astype(
        jnp.bfloat16
    )
    up_grads = (d_hidden * silu_gate).astype(jnp.bfloat16)
    return (mixed, logit_grads, gate_grads, up_grads, down_grads)


def solution(mesh):
    both = P(("dp", "sp"), None)
    return jax.shard_map(
        functools.partial(local, mesh.shape["dp"], mesh.shape["sp"]),
        mesh=mesh,
        in_specs=(P("dp", "sp"), P("dp", "sp"), P("sp", None), both, both, both),
        out_specs=(both, both, P("dp", "sp"), P("dp", "sp"), P("sp", "dp")),
        check_vma=False,
    )
```

profile of v0, /device:TPU:0, one launch (start us, length us, event | category | flops | bytes accessed | tf_op | source)
XLA Modules:
  0.0 121.9 jit_solution(460134272127837866)
XLA Ops:
  0.6 0.7 compare_reduce_fusion
  1.3 0.7 slice_compare_fusion
  2.0 0.8 fusion.14
  2.8 0.1 copy.49
  2.9 0.1 copy.55
  3.1 0.1 copy.50
  3.2 0.1 copy.48
  3.3 0.2 reduce-window.8
  3.5 0.1 add_reduce_fusion
  3.6 0.6 fusion.11.slot_choose_ref
  4.2 0.7 fusion.9.choose_ref
  4.9 0.1 copy.51
  5.0 0.7 fusion.13
  5.7 0.1 select_reduce_fusion
  5.8 0.7 copy.56.slot_weight_ref
  6.5 3.2 %fusion.hid_ref = bf16[256,2048]{1,0:T(8,128)(2,1)} fusion(bf16[256,2048]{1,0:T(8,128)(2,1)} %param.7, bf16[256,2048]{1,0:T(8,128)(2,1)} %param.6), kind=kLoop, calls=%fused_computation.5 | loop fusion | flops 4194304 | bytes 3145728 | tf_op jit(solution)/shard_map/convert_element_type | solution.py:412
  9.7 0.0 copy-start.3
  9.7 0.0 copy-start
  9.7 0.0 copy-start.1
  9.7 94.1 %shard_map.101 = (f32[256,2048]{1,0:T(8,128)}, bf16[8,256,2048]{2,1,0:T(8,128)(2,1)}, bf16[8,4,64,768]{3,2,1,0:T(8,128)(2,1)}, bf16[128,6144]{1,0:T(8,128)(2,1)}, f32[128,1]{1,0:T(8,128)}) custom-call(bf16[256,2048]{1,0:T(8,128)(2,1)} %fusion.hid_ref, bf16[64,128]{1,0:T(8,128)(2,1)} %fusion.11.slot_choose_ref, f32[64,1]{1,0:T(8,128)} %copy.56.slot_weight_ref, ...), custom_call_target="tpu_custom_call" | custom-call | tf_op jit(solution)/shard_map/pallas_call | solution.py:354
  103.9 0.0 copy-done.3
  103.9 0.9 fusion.12
  104.7 0.1 copy.59
  104.8 0.1 copy.58
  104.9 0.6 pad_maximum_fusion
  105.5 0.0 copy-done
  105.5 0.0 copy-done.1
  105.5 4.1 %multiply_convert_fusion = (bf16[256,2048]{1,0:T(8,128)(2,1)}, bf16[256,2048]{1,0:T(8,128)(2,1)}) fusion(f32[256,2048]{1,0:T(8,128)} %get-tuple-element.12, bf16[256,2048]{1,0:T(8,128)(2,1)S(1)} %copy-done.1, bf16[256,2048]{1,0:T(8,128)(2,1)S(1)} %copy-done), kind=kLoop, calls=%fused_computation.13 | loop fusion | flops 7864320 | bytes 6291456 | tf_op jit(solution)/shard_map/convert_element_type | solution.py:433
  109.6 0.0 copy-done.4
  109.6 11.1 %fusion.15 = f32[2048,768]{1,0:T(8,128)} fusion(bf16[2048,2048]{1,0:T(8,128)(2,1)} %bitcast.9, bf16[2048,768]{1,0:T(8,128)(2,1)S(1)} %bitcast.10), kind=kOutput, calls=%fused_computation.31 | convolution fusion | flops 6442450944 | bytes 17825792 | tf_op jit(solution)/shard_map/dot_general | solution.py:396
  120.7 0.0 copy-done.2
  120.7 1.1 copy.61
  (3 shorter events, 0.0 us)
Async XLA Ops:
  9.7 94.2 %copy-start.3 = (f32[128,1]{1,0:T(8,128)S(1)}, f32[128,1]{1,0:T(8,128)}, u32[]{:S(2)}) copy-start(f32[128,1]{1,0:T(8,128)} %get-tuple-element.28.weight_ref) | copy-start | bytes 1540
  9.7 95.8 %copy-start = (bf16[256,2048]{1,0:T(8,128)(2,1)S(1)}, bf16[256,2048]{1,0:T(8,128)(2,1)}, u32[]{:S(2)}) copy-start(bf16[256,2048]{1,0:T(8,128)(2,1)} %param.7) | copy-start | bytes 3145732
  9.7 95.8 %copy-start.1 = (bf16[256,2048]{1,0:T(8,128)(2,1)S(1)}, bf16[256,2048]{1,0:T(8,128)(2,1)}, u32[]{:S(2)}) copy-start(bf16[256,2048]{1,0:T(8,128)(2,1)} %param.6) | copy-start | bytes 3145732
  105.5 4.1 %copy-start.4 = (bf16[8,4,64,768]{3,2,1,0:T(8,128)(2,1)S(1)}, bf16[8,4,64,768]{3,2,1,0:T(8,128)(2,1)}, u32[]{:S(2)}) copy-start(bf16[8,4,64,768]{3,2,1,0:T(8,128)(2,1)} %get-tuple-element.14) | copy-start | bytes 9437188
  109.6 11.1 %copy-start.2 = (bf16[128,6144]{1,0:T(8,128)(2,1)S(1)}, bf16[128,6144]{1,0:T(8,128)(2,1)}, u32[]{:S(2)}) copy-start(bf16[128,6144]{1,0:T(8,128)(2,1)} %get-tuple-element.38) | copy-start | bytes 4718596
where the time goes:
time: 122 us
  Pallas kernels  94.1 us (77%)
  other arithmetic  12.6 us (10%)
  matrix products  11.1 us (9%)
  local copies, waits for them, and re-layouts  3.38 us (3%)
    pallas_call x1, Pallas kernels, exchange(): pl.pallas_call(functools.partial(exchange_kernel, n_dp, n_sp), out_shape=...  94.1 us
    dot_general x1, matrix products, contract_rows(): lax.dot_general(left, right, (((0,), (0,)), ((), ())), preferred_element_...  11.1 us
    convert_element_type x1, other arithmetic, local(): up_grads = (d_hidden * silu_gate).astype(jnp.bfloat16)  4.12 us
    convert_element_type x1, other arithmetic, local(): hidden = (silu_gate * up_wide).astype(jnp.bfloat16)  3.18 us

commit v1 on v0

v1 whole, which is shorter than its diff:
```python
import functools
import math

import jax
import jax.numpy as jnp
from jax import lax
from jax.experimental import pallas as pl
from jax.experimental.pallas import tpu as pltpu
from jax.sharding import PartitionSpec as P

MESH = pl.DeviceIdType.MESH
PIECES = 4


def fused_kernel(
    n_dp, n_sp, ids_ref, logit_ref, gate_hbm, up_hbm, w_ref, dout_hbm,
    mixed_ref, lgrad_ref, ggrad_ref, ugrad_ref, down_ref,
    gate, up, dout, hall, dall, dcyc, part, rs_ref, wcol, wrow,
    choose_slot, slot_weight, choose_tok, token_weight, wgrad,
    load_sem, wsem, local_sem, right_send, left_send, pair_send, hrecv, asend, arecv,
    gsend, grecv, bsend, brecv, rsend, rrecv, fsend, frecv, mate_send,
):
    f32, bf = jnp.float32, jnp.bfloat16
    dp, sp = lax.axis_index("dp"), lax.axis_index("sp")
    chips = n_dp // 2
    chip, core = lax.div(dp, 2), lax.rem(dp, 2)
    partner = chip * 2 + 1 - core
    slots, hid_width = gate.shape
    tokens, width = dout.shape
    slot_rows = dcyc.shape[1]
    block = width // n_dp
    rows = slots // PIECES
    tn = wcol.shape[2]
    th = wrow.shape[1]
    n_col, n_row = width // tn, hid_width // th

    barrier = pltpu.get_barrier_semaphore()
    for off in range(1, n_dp):
        pl.semaphore_signal(barrier, inc=1, device_id={"dp": lax.rem(dp + off, n_dp)}, device_id_type=MESH)
    for off in range(1, n_sp):
        pl.semaphore_signal(barrier, inc=1, device_id={"sp": lax.rem(sp + off, n_sp)}, device_id_type=MESH)

    def piece_rows(p):
        return slice(p * rows, (p + 1) * rows)

    def gate_load(p):
        return pltpu.make_async_copy(gate_hbm.at[piece_rows(p)], gate.at[piece_rows(p)], load_sem.at[2 * p])

    def up_load(p):
        return pltpu.make_async_copy(up_hbm.at[piece_rows(p)], up.at[piece_rows(p)], load_sem.at[2 * p + 1])

    dout_load = pltpu.make_async_copy(dout_hbm, dout, load_sem.at[2 * PIECES])

    def col_load(step, slot):
        return pltpu.make_async_copy(
            w_ref.at[:, pl.ds(pl.multiple_of(step * tn, tn), tn)], wcol.at[slot], wsem.at[slot]
        )

    def row_load(step, slot):
        return pltpu.make_async_copy(
            w_ref.at[pl.ds(pl.multiple_of(step * th, th), th), :], wrow.at[slot], wsem.at[2 + slot]
        )

    gate_load(0).start()
    up_load(0).start()
    dout_load.start()
    for p in range(1, PIECES):
        gate_load(p).start()
        up_load(p).start()
    col_load(0, 0).start()
    row_load(0, 0).start()

    def remote(src, dst, send, recv, **where):
        return pltpu.make_async_remote_copy(
            src_ref=src, dst_ref=dst, send_sem=send, recv_sem=recv, device_id=where, device_id_type=MESH
        )

    def arrived(ref, sem):
        pltpu.make_async_copy(ref, ref, sem).wait()

    def block_cols(index):
        return pl.ds(pl.multiple_of(index * block, block), block)

    zero = (ids_ref[...] == 0).astype(f32)
    first, second = zero[0:1, :], zero[1:2, :]
    routed = jnp.maximum(first, second)
    logits = logit_ref[...]
    own_logit = jnp.where(first > 0.0, logits[0:1, :], logits[1:2, :])
    other_logit = jnp.where(first > 0.0, logits[1:2, :], logits[0:1, :])
    weight = routed * jax.nn.sigmoid(own_logit - other_logit)
    along = lax.broadcasted_iota(jnp.int32, (tokens, tokens), 0)
    across = lax.broadcasted_iota(jnp.int32, (tokens, tokens), 1)
    before = jnp.where(along <= across, 1.0, 0.0).astype(bf)
    rank = jnp.dot(jnp.broadcast_to(routed, (16, tokens)).astype(bf), before, preferred_element_type=f32)[0:1, :] - 1.0
    chooser = jnp.where(along.astype(f32) == rank, 1.0, 0.0) * routed
    choose_slot[...] = chooser[:slot_rows, :].astype(bf)
    slot_weight[...] = jnp.sum(chooser[:slot_rows, :] * weight, axis=1, keepdims=True)
    choose_tok[...] = jnp.transpose(chooser).astype(bf)
    token_weight[...] = jnp.transpose(jnp.broadcast_to(weight, (tokens, tokens)))

    def make_hidden(p):
        gate_load(p).wait()
        up_load(p).wait()

        def step(i, carry):
            here = pl.ds(pl.multiple_of(p * rows + i * 16, 16), 16)
            gate_wide = gate[here, :].astype(f32)
            silu = gate_wide * jax.nn.sigmoid(gate_wide)
            hall[dp, here, :] = (silu * up[here, :].astype(f32)).astype(bf)
            return carry

        lax.fori_loop(0, rows // 16, step, 0)

    def piece(index, p):
        return hall.at[index, piece_rows(p)]

    def h_send(index, p, to, send):
        return remote(piece(index, p), piece(index, p), send, hrecv.at[PIECES * index + p], dp=to)

    def h_wait(index, p):
        arrived(piece(index, p), hrecv.at[PIECES * index + p])

    def h_right(index, p, step):
        return h_send(index, p, dp + 2, right_send.at[PIECES * step + p])

    def h_left(index, p, step):
        return h_send(index, p, dp - 2, left_send.at[PIECES * step + p])

    def h_pair(index, p):
        return h_send(index, p, partner, pair_send.at[PIECES * lax.div(index, 2) + p])

    def send_own(p):
        @pl.when(chip + 1 < chips)
        def _():
            h_right(dp, p, 0).start()

        @pl.when(chip >= 1)
        def _():
            h_left(dp, p, 0).start()

        h_pair(dp, p).start()

    def a_send(apart, to_core):
        other = 2 * lax.rem(chip + apart, chips) + to_core
        return remote(
            dcyc.at[sp, :, block_cols(other)], dall.at[2 * (chips - apart) + core, sp],
            asend.at[2 * apart + to_core], arecv.at[2 * (chips - apart) + core], dp=other,
        )

    away = [(apart, to_core) for apart in range(1, chips) for to_core in range(2)]

    make_hidden(0)
    pl.semaphore_wait(barrier, n_dp - 1 + n_sp - 1)
    send_own(0)

    dout_load.wait()

    def slot_step(step, carry):
        cols = pl.ds(pl.multiple_of(step * tn, tn), tn)
        picked = jnp.dot(choose_slot[...], dout[:, cols], preferred_element_type=f32)
        dcyc[sp, :, cols] = (slot_weight[...] * picked).astype(bf)
        return carry

    lax.fori_loop(0, n_col, slot_step, 0)

    relayed = n_sp == 4
    if relayed:
        near = [sp + 1 - 2 * lax.rem(sp, 2), lax.rem(sp + 2, 4)]
    else:
        near = [lax.rem(sp + off, n_sp) for off in range(1, n_sp)]
    ways = range(len(near))
    half_rows, half_dp = slot_rows // 2, (n_dp - 2) // 2

    def g_send(way):
        return remote(dcyc.at[sp], dcyc.at[sp], gsend.at[way], grecv.at[sp], sp=near[way])

    def b_send(way):
        return remote(dall.at[2:, sp], dall.at[2:, sp], bsend.at[way], brecv.at[sp], sp=near[way])

    def g_half(source, way):
        return dcyc.at[source, way * half_rows:(way + 1) * half_rows]

    def b_half(source, way):
        return dall.at[2 + way * half_dp:2 + (way + 1) * half_dp, source]

    def g_pass(way):
        held = g_half(near[way], way)
        return remote(held, held, fsend.at[way], frecv.at[way], sp=near[1 - way])

    def b_pass(way):
        held = b_half(near[way], way)
        return remote(held, held, fsend.at[2 + way], frecv.at[2 + way], sp=near[1 - way])

    for way in ways:
        g_send(way).start()
    for p in range(1, PIECES):
        make_hidden(p)
        send_own(p)
    for apart, to_core in away:
        a_send(apart, to_core).start()

    def r_send(step, off):
        other = lax.rem(sp + off, n_sp)
        cols = pl.ds(pl.multiple_of(step * tn, tn), tn)
        return remote(
            part.at[other, :, cols], rs_ref.at[sp, :, cols],
            rsend.at[step, off], rrecv.at[step, sp], sp=other,
        )

    def half_cols(step, way):
        half = tn // 2
        return pl.ds(pl.multiple_of(step * tn + way * half, half), half)

    def r_hop(step, way, kind):
        cols = half_cols(step, way)
        src = [part.at[near[way], :, cols], part.at[3 - sp, :, cols], rs_ref.at[3, :, cols]][kind]
        return remote(
            src, rs_ref.at[kind, :, cols], rsend.at[step, 2 * kind + way], rrecv.at[step, 2 * kind + way],
            sp=near[1 - way if kind == 2 else way],
        )

    def r_arrived(step, way, kind):
        arrived(rs_ref.at[kind, :, half_cols(step, way)], rrecv.at[step, 2 * kind + way])

    def fold_step(step, carry):
        for way in range(2):
            cols = half_cols(step, way)
            r_arrived(step, way, 1)
            rs_ref[3, :, cols] = (
                part[near[1 - way], :, cols].astype(f32) + rs_ref[1, :, cols].astype(f32)
            ).astype(bf)
            r_hop(step, way, 2).start()
        return carry

    def col_step(step, carry):
        slot = lax.rem(step, 2)

        @pl.when(step + 1 < n_col)
        def _():
            col_load(step + 1, 1 - slot).start()

        col_load(step, slot).wait()
        cols = pl.ds(pl.multiple_of(step * tn, tn), tn)
        product = jnp.dot(hall[dp], wcol[slot], preferred_element_type=f32)
        part[:, :, cols] = product.astype(bf).reshape(n_sp, slot_rows, tn)
        if relayed:
            for kind in (1, 0):
                for way in range(2):
                    r_hop(step, way, kind).start()
        else:
            for off in range(1, n_sp):
                r_send(step, off).start()
        return carry

    lax.fori_loop(0, n_col, col_step, 0)

    def relay(step, p):
        @pl.when(chip - step >= 0)
        def _():
            index = dp - 2 * step
            h_wait(index, p)

            @pl.when(chip + 1 < chips)
            def _():
                h_right(index, p, step).start()

            h_pair(index, p).start()

        @pl.when(chip + step < chips)
        def _():
            index = dp + 2 * step
            h_wait(index, p)

            @pl.when(chip >= 1)
            def _():
                h_left(index, p, step).start()

            h_pair(index, p).start()

    last = chips - 1
    for p in range(PIECES - 1):
        if last > 1:
            relay(1, p)
    for way in ways:
        arrived(dcyc.at[near[way]], grecv.at[near[way]])
        if relayed:
            g_pass(way).start()
    if last > 1:
        relay(1, PIECES - 1)

    if relayed:
        lax.fori_loop(0, n_col, fold_step, 0)

    for slot in range(2, n_dp):
        arrived(dall.at[slot, sp], arecv.at[slot])
    for way in ways:
        b_send(way).start()

    if relayed:
        for way in ways:
            arrived(g_half(3 - sp, way), frecv.at[way])

    own_copy = pltpu.make_async_copy(dcyc.at[:, :, block_cols(dp)], dall.at[core], local_sem.at[0])
    mate_copy = remote(
        dcyc.at[:, :, block_cols(partner)], dall.at[core], mate_send.at[0], arecv.at[core], dp=partner
    )
    own_copy.start()
    mate_copy.start()

    def row_step(step, carry):
        slot = lax.rem(step, 2)

        @pl.when(step + 1 < n_row)
        def _():
            row_load(step + 1, 1 - slot).start()

        row_load(step, slot).wait()
        cols = pl.ds(pl.multiple_of(step * th, th), th)
        d_hidden = lax.dot_general(
            dcyc[...].reshape(slots, width), wrow[slot], (((1,), (1,)), ((), ())), preferred_element_type=f32
        )
        gate_wide, up_wide = gate[:, cols].astype(f32), up[:, cols].astype(f32)
        sigma = jax.nn.sigmoid(gate_wide)
        ggrad_ref[:, cols] = (d_hidden * up_wide * sigma * (1.0 + gate_wide * (1.0 - sigma))).astype(bf)
        ugrad_ref[:, cols] = (d_hidden * (gate_wide * sigma)).astype(bf)
        return carry

    for p in range(PIECES):
        lax.fori_loop(p * n_row // PIECES, (p + 1) * n_row // PIECES, row_step, 0)
        if last > 2:
            relay(2, p)

    tw = min(256, hid_width)
    half_slots, half_sp = slots // 2, n_sp // 2

    def down_pass(source, half, initial):
        rel = lax.rem(source - chip + chips, chips)
        span, here, owners = slots, slice(None), slice(None)
        if half is not None:
            span = half_slots
            here, owners = slice(half * half_slots, (half + 1) * half_slots), slice(half * half_sp, (half + 1) * half_sp)

        def step(i, carry):
            cols = pl.ds(pl.multiple_of(i * tw, tw), tw)
            product = lax.dot_general(
                hall[pl.ds(2 * source, 2), here, cols].reshape(2 * span, tw),
                dall[pl.ds(2 * rel, 2), owners].reshape(2 * span, block),
                (((0,), (0,)), ((), ())), preferred_element_type=f32,
            )
            if initial:
                down_ref[cols, :] = product
            else:
                down_ref[cols, :] += product
            return carry

        lax.fori_loop(0, hid_width // tw, step, 0)

    own_copy.wait()
    arrived(dall.at[1 - core], arecv.at[1 - core])
    for p in range(PIECES):
        h_wait(partner, p)
    down_pass(chip, None, True)

    wgrad[...] = jnp.zeros_like(wgrad)

    def mix_step(step, carry):
        cols = pl.ds(pl.multiple_of(step * tn, tn), tn)
        total = part[sp, :, cols].astype(f32)
        if relayed:
            for kind in (0, 2):
                for way in range(2):
                    r_arrived(step, way, kind)
                total = total + rs_ref[kind, :, cols].astype(f32)
        else:
            for off in range(1, n_sp):
                other = lax.rem(sp + off, n_sp)
                arrived(rs_ref.at[other, :, cols], rrecv.at[step, other])
                total = total + rs_ref[other, :, cols].astype(f32)
        high = total.astype(bf)
        low = (total - high.astype(f32)).astype(bf)
        choose = choose_tok[:, :slot_rows]
        token_out = jnp.dot(choose, high, preferred_element_type=f32) + jnp.dot(
            choose, low, preferred_element_type=f32
        )
        mixed_ref[:, cols] = (token_weight[:, 0:1] * token_out).astype(bf)
        wgrad[...] += jnp.sum(dout[:, cols].astype(f32) * token_out, axis=1, keepdims=True)
        if relayed:
            for kind in range(3):
                for way in range(2):
                    r_hop(step, way, kind).wait_send()
        else:
            for off in range(1, n_sp):
                r_send(step, off).wait_send()
        return carry

    lax.fori_loop(0, n_col, mix_step, 0)

    slope = jnp.transpose(jnp.broadcast_to(wgrad[...], (tokens, tokens)))[0:1, :] * weight * (1.0 - weight)
    first_col = jnp.where(first > 0.0, slope, -slope)
    lgrad_ref[0:1, :] = first_col
    lgrad_ref[1:2, :] = -first_col

    for way in ways:
        arrived(dall.at[2:, near[way]], brecv.at[near[way]])
        if relayed:
            b_pass(way).start()

    for step in range(3, last):
        for p in range(PIECES):
            relay(step, p)

    if relayed:
        for way in ways:
            arrived(b_half(3 - sp, way), frecv.at[2 + way])

    def down_step(index, carry):
        source = chip + (lax.div(index, 2) + 1) * (2 * lax.rem(index, 2) - 1)

        @pl.when((source >= 0) & (source < chips))
        def _():
            for p in range(PIECES):
                h_wait(2 * source + 1 - core, p)
            down_pass(source, None, False)

        return carry

    if last > 1:
        lax.fori_loop(0, 2 * (last - 1), down_step, 0)

    if last > 0:
        @pl.when((chip == 0) | (chip == last))
        def _():
            source = last - chip
            for half in range(2):
                mine = range(half * PIECES // 2, (half + 1) * PIECES // 2)
                for p in mine:
                    h_wait(2 * source + core, p)
                    h_pair(2 * source + core, p).start()
                for p in mine:
                    h_wait(2 * source + 1 - core, p)
                down_pass(source, half, False)

    mate_copy.wait_send()
    for way in ways:
        g_send(way).wait_send()
        b_send(way).wait_send()
        if relayed:
            g_pass(way).wait_send()
            b_pass(way).wait_send()
    for apart, to_core in away:
        a_send(apart, to_core).wait_send()
    for step in range(chips):
        for p in range(PIECES):
            @pl.when((chip - step >= 0) & (chip + 1 < chips))
            def _():
                h_right(dp, p, step).wait_send()

            @pl.when((chip + step < chips) & (chip >= 1))
            def _():
                h_left(dp, p, step).wait_send()

            h_send(dp, p, partner, pair_send.at[PIECES * step + p]).wait_send()


def fused(n_dp, n_sp, ids, logits, gate_pre, up_pre, w_down, d_out):
    slots, hid_width = gate_pre.shape
    tokens, width = d_out.shape
    slot_rows = slots // n_sp
    block = width // n_dp
    tn, th = width // 8, min(256, hid_width)
    n_col = width // tn
    chips = n_dp // 2
    f32, bf = jnp.float32, jnp.bfloat16
    dma = pltpu.SemaphoreType.DMA
    hbm = pl.BlockSpec(memory_space=pl.ANY)
    vmem = pl.BlockSpec(memory_space=pltpu.VMEM)
    buffers = [
        ((slots, hid_width), bf), ((slots, hid_width), bf), ((tokens, width), bf),
        ((n_dp, slots, hid_width), bf), ((n_dp, n_sp, slot_rows, block), bf),
        ((n_sp, slot_rows, width), bf), ((n_sp, slot_rows, width), bf), ((n_sp, slot_rows, width), bf),
        ((2, hid_width, tn), bf), ((2, th, width), bf),
        ((slot_rows, tokens), bf), ((slot_rows, 1), f32), ((tokens, tokens), bf), ((tokens, tokens), f32),
        ((tokens, 1), f32),
    ]
    held = sum(math.prod(shape) * jnp.dtype(dtype).itemsize for shape, dtype in buffers)
    return pl.pallas_call(
        functools.partial(fused_kernel, n_dp, n_sp),
        out_shape=(
            pltpu.VMEM((tokens, width), bf),
            pltpu.VMEM((2, tokens), f32),
            pltpu.VMEM((slots, hid_width), bf),
            pltpu.VMEM((slots, hid_width), bf),
            pltpu.VMEM((hid_width, block), f32),
        ),
        in_specs=[vmem, vmem, hbm, hbm, hbm, hbm],
        out_specs=(vmem,) * 5,
        scratch_shapes=[pltpu.VMEM(shape, dtype) for shape, dtype in buffers] + [
            dma((2 * PIECES + 1,)),
            dma((4,)),
            dma((1,)),
            dma((PIECES * chips,)),
            dma((PIECES * chips,)),
            dma((PIECES * chips,)),
            dma((PIECES * n_dp,)),
            dma((n_dp,)),
            dma((n_dp,)),
            dma((n_sp,)),
            dma((n_sp,)),
            dma((n_sp,)),
            dma((n_sp,)),
            dma((n_col, max(n_sp, 6))),
            dma((n_col, max(n_sp, 6))),
            dma((4,)),
            dma((4,)),
            dma((1,)),
        ],
        compiler_params=pltpu.CompilerParams(
            collective_id=0, has_side_effects=True, vmem_limit_bytes=held + 4 * 1024 * 1024
        ),
    )(ids, logits, gate_pre, up_pre, w_down, d_out)


def local(n_dp, n_sp, gate_pre, up_pre, w_down, route_logits, expert_ids, d_out):
    mixed, slopes, gate_grads, up_grads, down_grads = fused(
        n_dp, n_sp, expert_ids.T, route_logits.T, gate_pre, up_pre, w_down, d_out
    )
    return (mixed, slopes.T, gate_grads, up_grads, down_grads)


def solution(mesh):
    both = P(("dp", "sp"), None)
    return jax.shard_map(
        functools.partial(local, mesh.shape["dp"], mesh.shape["sp"]),
        mesh=mesh,
        in_specs=(P("dp", "sp"), P("dp", "sp"), P("sp", None), both, both, both),
        out_specs=(both, both, P("dp", "sp"), P("dp", "sp"), P("sp", "dp")),
        check_vma=False,
    )
```

time: 122 us -> 111 us (0.910)
  other arithmetic: 12.6 us -> 0 us
  matrix products: 11.1 us -> 0 us
  local copies, waits for them, and re-layouts: 3.38 us -> 11.6 us
  Pallas kernels: 94.1 us -> 97.8 us
    dot_general x1 -> x0, matrix products: 11.1 us -> none  [contract_rows(): lax.dot_general(left, right, (((0,), (0,)), ((), ())), preferred_element_...]
    unnamed x11 -> x15, local copies, waits for them, and re-layouts: 1.16 us -> 11.6 us
    convert_element_type x5 -> x0, other arithmetic: 8.65 us -> none  [the longest x1 4.12 us: local(): up_grads = (d_hidden * silu_gate).astype(jnp.bfloat16)]
    pallas_call x1, Pallas kernels: 94.1 us -> 97.8 us  [fused(): pl.pallas_call(functools.partial(fused_kernel, n_dp, n_sp), out_shape=(pl...]
where the time goes in v1:
time: 111 us; the launch traced here: 110 us
  Pallas kernels  97.8 us (88%)
  local copies, waits for them, and re-layouts  11.6 us (10%)
    pallas_call x1, Pallas kernels, fused(): pl.pallas_call(functools.partial(fused_kernel, n_dp, n_sp), out_shape=(pl...  97.8 us
    unnamed x15, local copies, waits for them, and re-layouts  11.6 us

profile of v1, /device:TPU:0, one launch (start us, length us, event | category | flops | bytes accessed | tf_op | source)
XLA Modules:
  0.0 110.0 jit_solution(6132357477210919213)
XLA Ops:
  0.6 0.0 copy-start
  0.6 1.4 %copy-done = bf16[128,6144]{1,0:T(8,128)(2,1)S(1)} copy-done((bf16[128,6144]{1,0:T(8,128)(2,1)S(1)}, bf16[128,6144]{1,0:T(8,128)(2,1)}, u32[]{:S(2)}) %copy-start) | copy-done | bytes 1572888
  2.0 0.0 copy-start.1
  2.0 1.2 %copy-done.1 = bf16[256,2048]{1,0:T(8,128)(2,1)S(1)} copy-done((bf16[256,2048]{1,0:T(8,128)(2,1)S(1)}, bf16[256,2048]{1,0:T(8,128)(2,1)}, u32[]{:S(2)}) %copy-start.1) | copy-done | bytes 1048600
  3.3 0.0 copy-start.2
  3.3 1.2 %copy-done.2 = bf16[256,2048]{1,0:T(8,128)(2,1)S(1)} copy-done((bf16[256,2048]{1,0:T(8,128)(2,1)S(1)}, bf16[256,2048]{1,0:T(8,128)(2,1)}, u32[]{:S(2)}) %copy-start.2) | copy-done | bytes 1048600
  4.5 0.0 copy-start.3
  4.5 0.7 copy-done.3
  5.2 0.0 copy-start.4
  5.2 0.7 copy-done.4
  5.9 97.8 %shard_map.101 = (bf16[128,6144]{1,0:T(8,128)(2,1)S(1)}, f32[2,128]{1,0:T(2,128)S(1)}, bf16[256,2048]{1,0:T(8,128)(2,1)S(1)}, bf16[256,2048]{1,0:T(8,128)(2,1)S(1)}, f32[2048,768]{1,0:T(8,128)S(1)}) custom-call(s32[2,128]{1,0:T(2,128)S(1)} %bitcast.4, f32[2,128]{1,0:T(2,128)S(1)} %bitcast.5, bf16[256,2048]{1,0:T(8,128)(2,1)S(1)} %copy-done.1, ...), custom_call_target="tpu_custom_call" | custom-call | tf_op jit(solution)/shard_map/pallas_call | solution.py:486
  103.7 1.1 %copy.16 = bf16[128,6144]{1,0:T(8,128)(2,1)} copy(bf16[128,6144]{1,0:T(8,128)(2,1)S(1)} %get-tuple-element.15) | data formatting | bytes 3145728
  104.8 0.6 copy.17
  105.4 1.0 copy.18
  106.4 1.0 copy.19
  107.3 2.7 %copy.20 = f32[2048,768]{1,0:T(8,128)} copy(f32[2048,768]{1,0:T(8,128)S(1)} %get-tuple-element.19) | data formatting | bytes 12582912
Async XLA Ops:
  0.6 1.4 %copy-start = (bf16[128,6144]{1,0:T(8,128)(2,1)S(1)}, bf16[128,6144]{1,0:T(8,128)(2,1)}, u32[]{:S(2)}) copy-start(bf16[128,6144]{1,0:T(8,128)(2,1)} %dout_hbm.1) | copy-start | bytes 4718596
  2.0 1.2 %copy-start.1 = (bf16[256,2048]{1,0:T(8,128)(2,1)S(1)}, bf16[256,2048]{1,0:T(8,128)(2,1)}, u32[]{:S(2)}) copy-start(bf16[256,2048]{1,0:T(8,128)(2,1)} %gate_hbm.1) | copy-start | bytes 3145732
  3.3 1.2 %copy-start.2 = (bf16[256,2048]{1,0:T(8,128)(2,1)S(1)}, bf16[256,2048]{1,0:T(8,128)(2,1)}, u32[]{:S(2)}) copy-start(bf16[256,2048]{1,0:T(8,128)(2,1)} %up_hbm.1) | copy-start | bytes 3145732
  4.5 0.7 copy-start.3
  5.2 0.7 copy-start.4

commit v2 on v1

--- a/solution.py
+++ b/solution.py
@@ -330,7 +330,7 @@
         if last > 2:
             relay(2, p)
 
-    tw = min(256, hid_width)
+    wide = 256 if block % 256 == 0 else 128
     half_slots, half_sp = slots // 2, n_sp // 2
 
     def down_pass(source, half, initial):
@@ -340,20 +340,17 @@
             span = half_slots
             here, owners = slice(half * half_slots, (half + 1) * half_slots), slice(half * half_sp, (half + 1) * half_sp)
 
-        def step(i, carry):
-            cols = pl.ds(pl.multiple_of(i * tw, tw), tw)
+        left = hall[pl.ds(2 * source, 2), here].reshape(2 * span, hid_width)
+        for start in range(0, block, wide):
+            cols = slice(start, start + wide)
             product = lax.dot_general(
-                hall[pl.ds(2 * source, 2), here, cols].reshape(2 * span, tw),
-                dall[pl.ds(2 * rel, 2), owners].reshape(2 * span, block),
+                left, dall[pl.ds(2 * rel, 2), owners, :, cols].reshape(2 * span, wide),
                 (((0,), (0,)), ((), ())), preferred_element_type=f32,
             )
             if initial:
-                down_ref[cols, :] = product
+                down_ref[:, cols] = product
             else:
-                down_ref[cols, :] += product
-            return carry
-
-        lax.fori_loop(0, hid_width // tw, step, 0)
+                down_ref[:, cols] += product
 
     own_copy.wait()
     arrived(dall.at[1 - core], arecv.at[1 - core])
@@ -482,16 +479,14 @@
         ((slot_rows, tokens), bf), ((slot_rows, 1), f32), ((tokens, tokens), bf), ((tokens, tokens), f32),
         ((tokens, 1), f32),
     ]
-    held = sum(math.prod(shape) * jnp.dtype(dtype).itemsize for shape, dtype in buffers)
+    results = [
+        ((tokens, width), bf), ((2, tokens), f32), ((slots, hid_width), bf), ((slots, hid_width), bf),
+        ((hid_width, block), f32),
+    ]
+    kept = sum(math.prod(shape) * jnp.dtype(dtype).itemsize for shape, dtype in results)
     return pl.pallas_call(
         functools.partial(fused_kernel, n_dp, n_sp),
-        out_shape=(
-            pltpu.VMEM((tokens, width), bf),
-            pltpu.VMEM((2, tokens), f32),
-            pltpu.VMEM((slots, hid_width), bf),
-            pltpu.VMEM((slots, hid_width), bf),
-            pltpu.VMEM((hid_width, block), f32),
-        ),
+        out_shape=tuple(pltpu.VMEM(shape, dtype) for shape, dtype in results),
         in_specs=[vmem, vmem, hbm, hbm, hbm, hbm],
         out_specs=(vmem,) * 5,
         scratch_shapes=[pltpu.VMEM(shape, dtype) for shape, dtype in buffers] + [
@@ -515,15 +510,36 @@
             dma((1,)),
         ],
         compiler_params=pltpu.CompilerParams(
-            collective_id=0, has_side_effects=True, vmem_limit_bytes=held + 4 * 1024 * 1024
+            collective_id=0, has_side_effects=True, vmem_limit_bytes=62 * 1024 * 1024 - kept
         ),
     )(ids, logits, gate_pre, up_pre, w_down, d_out)
 
 
+def emit_kernel(*refs):
+    count = len(refs) // 2
+    sems = refs[-1]
+    copies = [pltpu.make_async_copy(refs[i], refs[count + i], sems.at[i]) for i in range(count)]
+    for copy in copies:
+        copy.start()
+    for copy in copies:
+        copy.wait()
+
+
+def emit(*arrays):
+    return pl.pallas_call(
+        emit_kernel,
+        out_shape=tuple(jax.ShapeDtypeStruct(array.shape, array.dtype) for array in arrays),
+        in_specs=[pl.BlockSpec(memory_space=pltpu.VMEM)] * len(arrays),
+        out_specs=(pl.BlockSpec(memory_space=pl.ANY),) * len(arrays),
+        scratch_shapes=[pltpu.SemaphoreType.DMA((len(arrays),))],
+        compiler_params=pltpu.CompilerParams(vmem_limit_bytes=1024 * 1024),
+    )(*[pltpu.with_memory_space_constraint(array, pltpu.VMEM) for array in arrays])
+
+
 def local(n_dp, n_sp, gate_pre, up_pre, w_down, route_logits, expert_ids, d_out):
-    mixed, slopes, gate_grads, up_grads, down_grads = fused(
+    mixed, slopes, gate_grads, up_grads, down_grads = emit(*fused(
         n_dp, n_sp, expert_ids.T, route_logits.T, gate_pre, up_pre, w_down, d_out
-    )
+    ))
     return (mixed, slopes.T, gate_grads, up_grads, down_grads)
 
 

time: 111 us -> 98.1 us (0.88)
  local copies, waits for them, and re-layouts: 11.6 us -> 0 us
    unnamed x15 -> x0, local copies, waits for them, and re-layouts: 11.6 us -> none
    pallas_call x1 -> x2, Pallas kernels: 97.8 us -> 97.1 us  [the longest x1 93.1 us: fused(): pl.pallas_call(functools.partial(fused_kernel, n_dp, n_sp), out_shape=tup...]
where the time goes in v2:
time: 98.1 us; the launch traced here: 97.7 us
  Pallas kernels  97.1 us (99%)
    pallas_call x1, Pallas kernels, fused(): pl.pallas_call(functools.partial(fused_kernel, n_dp, n_sp), out_shape=tup...  93.1 us
    pallas_call x1, Pallas kernels, emit(): pl.pallas_call(emit_kernel, out_shape=tuple((jax.ShapeDtypeStruct(array.s...  3.96 us

profile of v2, /device:TPU:0, one launch (start us, length us, event | category | flops | bytes accessed | tf_op | source)
XLA Modules:
  0.0 97.7 jit_solution(624283991097610182)
XLA Ops:
  0.6 93.1 %shard_map.101 = (bf16[128,6144]{1,0:T(8,128)(2,1)S(1)}, f32[2,128]{1,0:T(2,128)S(1)}, bf16[256,2048]{1,0:T(8,128)(2,1)S(1)}, bf16[256,2048]{1,0:T(8,128)(2,1)S(1)}, f32[2048,768]{1,0:T(8,128)S(1)}) custom-call(s32[2,128]{1,0:T(2,128)} %bitcast.3, f32[2,128]{1,0:T(2,128)} %bitcast.4, bf16[256,2048]{1,0:T(8,128)(2,1)} %gate_hbm.1, bf16[256,2048]{1,0:T(8,128)(2,1)} %up_hbm.1, ...), custom_call_target="tpu_custom_call" | custom-call | tf_op jit(solution)/shard_map/pallas_call | solution.py:487
  93.7 4.0 %shard_map.102 = (bf16[128,6144]{1,0:T(8,128)(2,1)}, f32[2,128]{1,0:T(2,128)}, bf16[256,2048]{1,0:T(8,128)(2,1)}, bf16[256,2048]{1,0:T(8,128)(2,1)}, f32[2048,768]{1,0:T(8,128)}) custom-call(bf16[128,6144]{1,0:T(8,128)(2,1)S(1)} %get-tuple-element.15.refs_0_, f32[2,128]{1,0:T(2,128)S(1)} %get-tuple-element.16.refs_1_, ...), custom_call_target="tpu_custom_call" | custom-call | tf_op jit(solution)/shard_map/pallas_call | solution.py:529

commit v3 on v2

--- a/solution.py
+++ b/solution.py
@@ -9,13 +9,16 @@
 from jax.sharding import PartitionSpec as P
 
 MESH = pl.DeviceIdType.MESH
-PIECES = 4
+CUTS = (0, 1, 3, 5, 7, 8)
+PIECES = len(CUTS) - 1
+LATE = 2
+CHUNKS = 4
 
 
 def fused_kernel(
-    n_dp, n_sp, ids_ref, logit_ref, gate_hbm, up_hbm, w_ref, dout_hbm,
-    mixed_ref, lgrad_ref, ggrad_ref, ugrad_ref, down_ref,
-    gate, up, dout, hall, dall, dcyc, part, rs_ref, wcol, wrow,
+    n_dp, n_sp, ids_hbm, logit_hbm, gate_hbm, up_hbm, w_ref, dout_hbm,
+    mixed_ref, lgrad_ref, ggrad_ref, ugrad_ref, down_ref, late_hid, late_cot,
+    ids_ref, logit_ref, gate, up, dout, hall, dall, dcyc, part, rs_ref, wcol, wrow,
     choose_slot, slot_weight, choose_tok, token_weight, wgrad,
     load_sem, wsem, local_sem, right_send, left_send, pair_send, hrecv, asend, arecv,
     gsend, grecv, bsend, brecv, rsend, rrecv, fsend, frecv, mate_send,
@@ -29,40 +32,45 @@
     tokens, width = dout.shape
     slot_rows = dcyc.shape[1]
     block = width // n_dp
-    rows = slots // PIECES
+    bounds = [cut * slots // CUTS[-1] for cut in CUTS]
+    early = bounds[PIECES - LATE]
+    late = slots - early
     tn = wcol.shape[2]
     th = wrow.shape[1]
     n_col, n_row = width // tn, hid_width // th
 
+    def piece_rows(p):
+        return slice(bounds[p], bounds[p + 1])
+
+    def gate_load(p):
+        return pltpu.make_async_copy(gate_hbm.at[piece_rows(p)], gate.at[piece_rows(p)], load_sem.at[2 * p])
+
+    def up_load(p):
+        return pltpu.make_async_copy(up_hbm.at[piece_rows(p)], up.at[piece_rows(p)], load_sem.at[2 * p + 1])
+
+    ids_load = pltpu.make_async_copy(ids_hbm, ids_ref, load_sem.at[2 * PIECES + 1])
+    logit_load = pltpu.make_async_copy(logit_hbm, logit_ref, load_sem.at[2 * PIECES + 2])
+    dout_load = pltpu.make_async_copy(dout_hbm, dout, load_sem.at[2 * PIECES])
+
+    def col_load(step, slot):
+        return pltpu.make_async_copy(
+            w_ref.at[:, pl.ds(pl.multiple_of(step * tn, tn), tn)], wcol.at[slot], wsem.at[slot]
+        )
+
+    def row_load(step, slot):
+        return pltpu.make_async_copy(
+            w_ref.at[pl.ds(pl.multiple_of(step * th, th), th), :], wrow.at[slot], wsem.at[2 + slot]
+        )
+
+    gate_load(0).start()
+    up_load(0).start()
     barrier = pltpu.get_barrier_semaphore()
     for off in range(1, n_dp):
         pl.semaphore_signal(barrier, inc=1, device_id={"dp": lax.rem(dp + off, n_dp)}, device_id_type=MESH)
     for off in range(1, n_sp):
         pl.semaphore_signal(barrier, inc=1, device_id={"sp": lax.rem(sp + off, n_sp)}, device_id_type=MESH)
-
-    def piece_rows(p):
-        return slice(p * rows, (p + 1) * rows)
-
-    def gate_load(p):
-        return pltpu.make_async_copy(gate_hbm.at[piece_rows(p)], gate.at[piece_rows(p)], load_sem.at[2 * p])
-
-    def up_load(p):
-        return pltpu.make_async_copy(up_hbm.at[piece_rows(p)], up.at[piece_rows(p)], load_sem.at[2 * p + 1])
-
-    dout_load = pltpu.make_async_copy(dout_hbm, dout, load_sem.at[2 * PIECES])
-
-    def col_load(step, slot):
-        return pltpu.make_async_copy(
-            w_ref.at[:, pl.ds(pl.multiple_of(step * tn, tn), tn)], wcol.at[slot], wsem.at[slot]
-        )
-
-    def row_load(step, slot):
-        return pltpu.make_async_copy(
-            w_ref.at[pl.ds(pl.multiple_of(step * th, th), th), :], wrow.at[slot], wsem.at[2 + slot]
-        )
-
-    gate_load(0).start()
-    up_load(0).start()
+    ids_load.start()
+    logit_load.start()
     dout_load.start()
     for p in range(1, PIECES):
         gate_load(p).start()
@@ -81,6 +89,63 @@
     def block_cols(index):
         return pl.ds(pl.multiple_of(index * block, block), block)
 
+    def make_hidden(p):
+        gate_load(p).wait()
+        up_load(p).wait()
+
+        def step(i, carry):
+            here = pl.ds(pl.multiple_of(bounds[p] + i * 16, 16), 16)
+            gate_wide = gate[here, :].astype(f32)
+            silu = gate_wide * jax.nn.sigmoid(gate_wide)
+            hall[dp, here, :] = (silu * up[here, :].astype(f32)).astype(bf)
+            return carry
+
+        lax.fori_loop(0, (bounds[p + 1] - bounds[p]) // 16, step, 0)
+
+    def piece(index, p):
+        return hall.at[index, piece_rows(p)]
+
+    def h_send(index, p, to, send):
+        return remote(piece(index, p), piece(index, p), send, hrecv.at[PIECES * index + p], dp=to)
+
+    def h_wait(index, p):
+        arrived(piece(index, p), hrecv.at[PIECES * index + p])
+
+    def h_right(index, p, step):
+        return h_send(index, p, dp + 2, right_send.at[PIECES * step + p])
+
+    def h_left(index, p, step):
+        return h_send(index, p, dp - 2, left_send.at[PIECES * step + p])
+
+    def h_pair(index, p):
+        return h_send(index, p, partner, pair_send.at[PIECES * lax.div(index, 2) + p])
+
+    def send_own(p):
+        @pl.when(chip + 1 < chips)
+        def _():
+            h_right(dp, p, 0).start()
+
+        @pl.when(chip >= 1)
+        def _():
+            h_left(dp, p, 0).start()
+
+        h_pair(dp, p).start()
+
+    def a_send(apart, to_core):
+        other = 2 * lax.rem(chip + apart, chips) + to_core
+        return remote(
+            dcyc.at[sp, :, block_cols(other)], dall.at[2 * (chips - apart) + core, sp],
+            asend.at[2 * apart + to_core], arecv.at[2 * (chips - apart) + core], dp=other,
+        )
+
+    away = [(apart, to_core) for apart in range(1, chips) for to_core in range(2)]
+
+    make_hidden(0)
+    pl.semaphore_wait(barrier, n_dp - 1 + n_sp - 1)
+    send_own(0)
+
+    ids_load.wait()
+    logit_load.wait()
     zero = (ids_ref[...] == 0).astype(f32)
     first, second = zero[0:1, :], zero[1:2, :]
     routed = jnp.maximum(first, second)
@@ -98,61 +163,6 @@
     choose_tok[...] = jnp.transpose(chooser).astype(bf)
     token_weight[...] = jnp.transpose(jnp.broadcast_to(weight, (tokens, tokens)))
 
-    def make_hidden(p):
-        gate_load(p).wait()
-        up_load(p).wait()
-
-        def step(i, carry):
-            here = pl.ds(pl.multiple_of(p * rows + i * 16, 16), 16)
-            gate_wide = gate[here, :].astype(f32)
-            silu = gate_wide * jax.nn.sigmoid(gate_wide)
-            hall[dp, here, :] = (silu * up[here, :].astype(f32)).astype(bf)
-            return carry
-
-        lax.fori_loop(0, rows // 16, step, 0)
-
-    def piece(index, p):
-        return hall.at[index, piece_rows(p)]
-
-    def h_send(index, p, to, send):
-        return remote(piece(index, p), piece(index, p), send, hrecv.at[PIECES * index + p], dp=to)
-
-    def h_wait(index, p):
-        arrived(piece(index, p), hrecv.at[PIECES * index + p])
-
-    def h_right(index, p, step):
-        return h_send(index, p, dp + 2, right_send.at[PIECES * step + p])
-
-    def h_left(index, p, step):
-        return h_send(index, p, dp - 2, left_send.at[PIECES * step + p])
-
-    def h_pair(index, p):
-        return h_send(index, p, partner, pair_send.at[PIECES * lax.div(index, 2) + p])
-
-    def send_own(p):
-        @pl.when(chip + 1 < chips)
-        def _():
-            h_right(dp, p, 0).start()
-
-        @pl.when(chip >= 1)
-        def _():
-            h_left(dp, p, 0).start()
-
-        h_pair(dp, p).start()
-
-    def a_send(apart, to_core):
-        other = 2 * lax.rem(chip + apart, chips) + to_core
-        return remote(
-            dcyc.at[sp, :, block_cols(other)], dall.at[2 * (chips - apart) + core, sp],
-            asend.at[2 * apart + to_core], arecv.at[2 * (chips - apart) + core], dp=other,
-        )
-
-    away = [(apart, to_core) for apart in range(1, chips) for to_core in range(2)]
-
-    make_hidden(0)
-    pl.semaphore_wait(barrier, n_dp - 1 + n_sp - 1)
-    send_own(0)
-
     dout_load.wait()
 
     def slot_step(step, carry):
@@ -193,11 +203,13 @@
 
     for way in ways:
         g_send(way).start()
+    for apart, to_core in away:
+        a_send(apart, to_core).start()
     for p in range(1, PIECES):
         make_hidden(p)
         send_own(p)
-    for apart, to_core in away:
-        a_send(apart, to_core).start()
+    late_hid[...] = jnp.zeros_like(late_hid)
+    late_cot[...] = jnp.zeros_like(late_cot)
 
     def r_send(step, off):
         other = lax.rem(sp + off, n_sp)
@@ -243,16 +255,21 @@
         cols = pl.ds(pl.multiple_of(step * tn, tn), tn)
         product = jnp.dot(hall[dp], wcol[slot], preferred_element_type=f32)
         part[:, :, cols] = product.astype(bf).reshape(n_sp, slot_rows, tn)
-        if relayed:
-            for kind in (1, 0):
+        return carry
+
+    lax.fori_loop(0, n_col, col_step, 0)
+
+    def part_sends(kind):
+        def step_sends(step, carry):
+            if relayed:
                 for way in range(2):
                     r_hop(step, way, kind).start()
-        else:
-            for off in range(1, n_sp):
-                r_send(step, off).start()
-        return carry
-
-    lax.fori_loop(0, n_col, col_step, 0)
+            else:
+                for off in range(1, n_sp):
+                    r_send(step, off).start()
+            return carry
+
+        lax.fori_loop(0, n_col, step_sends, 0)
 
     def relay(step, p):
         @pl.when(chip - step >= 0)
@@ -278,23 +295,27 @@
             h_pair(index, p).start()
 
     last = chips - 1
-    for p in range(PIECES - 1):
-        if last > 1:
-            relay(1, p)
+    for slot in range(2, n_dp):
+        arrived(dall.at[slot, sp], arecv.at[slot])
+    for way in ways:
+        b_send(way).start()
     for way in ways:
         arrived(dcyc.at[near[way]], grecv.at[near[way]])
         if relayed:
             g_pass(way).start()
-    if last > 1:
-        relay(1, PIECES - 1)
-
+    part_sends(1)
+    for p in range(PIECES - LATE):
+        if last > 1:
+            relay(1, p)
+    for way in ways:
+        arrived(dall.at[2:, near[way]], brecv.at[near[way]])
+        if relayed:
+            b_pass(way).start()
     if relayed:
-        lax.fori_loop(0, n_col, fold_step, 0)
-
-    for slot in range(2, n_dp):
-        arrived(dall.at[slot, sp], arecv.at[slot])
-    for way in ways:
-        b_send(way).start()
+        part_sends(0)
+    for p in range(PIECES - LATE, PIECES):
+        if last > 1:
+            relay(1, p)
 
     if relayed:
         for way in ways:
@@ -329,22 +350,21 @@
         lax.fori_loop(p * n_row // PIECES, (p + 1) * n_row // PIECES, row_step, 0)
         if last > 2:
             relay(2, p)
+        if relayed and p == 1:
+            lax.fori_loop(0, n_col, fold_step, 0)
 
     wide = 256 if block % 256 == 0 else 128
-    half_slots, half_sp = slots // 2, n_sp // 2
-
-    def down_pass(source, half, initial):
+
+    def cotangents(source, cols):
         rel = lax.rem(source - chip + chips, chips)
-        span, here, owners = slots, slice(None), slice(None)
-        if half is not None:
-            span = half_slots
-            here, owners = slice(half * half_slots, (half + 1) * half_slots), slice(half * half_sp, (half + 1) * half_sp)
-
-        left = hall[pl.ds(2 * source, 2), here].reshape(2 * span, hid_width)
+        return dall[pl.ds(2 * rel, 2), :, :, cols].reshape(2, slots, -1)
+
+    def down_pass(source, span, initial):
+        left = hall[pl.ds(2 * source, 2), :span].reshape(2 * span, hid_width)
         for start in range(0, block, wide):
             cols = slice(start, start + wide)
             product = lax.dot_general(
-                left, dall[pl.ds(2 * rel, 2), owners, :, cols].reshape(2 * span, wide),
+                left, cotangents(source, cols)[:, :span].reshape(2 * span, wide),
                 (((0,), (0,)), ((), ())), preferred_element_type=f32,
             )
             if initial:
@@ -356,7 +376,7 @@
     arrived(dall.at[1 - core], arecv.at[1 - core])
     for p in range(PIECES):
         h_wait(partner, p)
-    down_pass(chip, None, True)
+    down_pass(chip, slots, True)
 
     wgrad[...] = jnp.zeros_like(wgrad)
 
@@ -390,52 +410,46 @@
                 r_send(step, off).wait_send()
         return carry
 
+    for step in range(3, last):
+        for p in range(PIECES):
+            relay(step, p)
+
+    if relayed:
+        for way in ways:
+            arrived(b_half(3 - sp, way), frecv.at[2 + way])
+
+    def down_step(index, carry):
+        source = chip + (lax.div(index, 2) + 1) * (2 * lax.rem(index, 2) - 1)
+
+        @pl.when((source >= 0) & (source < chips))
+        def _():
+            for p in range(PIECES):
+                h_wait(2 * source + 1 - core, p)
+            down_pass(source, slots, False)
+
+        return carry
+
+    if last > 1:
+        lax.fori_loop(0, 2 * (last - 1), down_step, 0)
+
+    ends = (chip == 0) | (chip == last)
+    far = last - chip
+
+    def forward(p):
+        @pl.when(ends)
+        def _():
+            h_wait(2 * far + core, p)
+            h_pair(2 * far + core, p).start()
+
+    for p in range(2):
+        forward(p)
+
     lax.fori_loop(0, n_col, mix_step, 0)
 
     slope = jnp.transpose(jnp.broadcast_to(wgrad[...], (tokens, tokens)))[0:1, :] * weight * (1.0 - weight)
     first_col = jnp.where(first > 0.0, slope, -slope)
     lgrad_ref[0:1, :] = first_col
     lgrad_ref[1:2, :] = -first_col
-
-    for way in ways:
-        arrived(dall.at[2:, near[way]], brecv.at[near[way]])
-        if relayed:
-            b_pass(way).start()
-
-    for step in range(3, last):
-        for p in range(PIECES):
-            relay(step, p)
-
-    if relayed:
-        for way in ways:
-            arrived(b_half(3 - sp, way), frecv.at[2 + way])
-
-    def down_step(index, carry):
-        source = chip + (lax.div(index, 2) + 1) * (2 * lax.rem(index, 2) - 1)
-
-        @pl.when((source >= 0) & (source < chips))
-        def _():
-            for p in range(PIECES):
-                h_wait(2 * source + 1 - core, p)
-            down_pass(source, None, False)
-
-        return carry
-
-    if last > 1:
-        lax.fori_loop(0, 2 * (last - 1), down_step, 0)
-
-    if last > 0:
-        @pl.when((chip == 0) | (chip == last))
-        def _():
-            source = last - chip
-            for half in range(2):
-                mine = range(half * PIECES // 2, (half + 1) * PIECES // 2)
-                for p in mine:
-                    h_wait(2 * source + core, p)
-                    h_pair(2 * source + core, p).start()
-                for p in mine:
-                    h_wait(2 * source + 1 - core, p)
-                down_pass(source, half, False)
 
     mate_copy.wait_send()
     for way in ways:
@@ -446,16 +460,41 @@
             b_pass(way).wait_send()
     for apart, to_core in away:
         a_send(apart, to_core).wait_send()
+
+    def sent(step, p):
+        @pl.when((chip - step >= 0) & (chip + 1 < chips))
+        def _():
+            h_right(dp, p, step).wait_send()
+
+        @pl.when((chip + step < chips) & (chip >= 1))
+        def _():
+            h_left(dp, p, step).wait_send()
+
+    for p in range(PIECES):
+        for step in range(last):
+            sent(step, p)
+
+    for p in range(2, PIECES - LATE):
+        forward(p)
+
+    @pl.when(ends)
+    def _():
+        for p in range(PIECES - LATE):
+            h_wait(2 * far + 1 - core, p)
+        down_pass(far, early, False)
+        late_cot[...] = cotangents(far, slice(None))[:, early:].reshape(2 * late, block)
+
+    for p in range(PIECES - LATE, PIECES):
+        forward(p)
+
+    @pl.when(ends)
+    def _():
+        for p in range(PIECES - LATE, PIECES):
+            h_wait(2 * far + 1 - core, p)
+        late_hid[...] = hall[pl.ds(2 * far, 2), early:].reshape(2 * late, hid_width)
+
     for step in range(chips):
         for p in range(PIECES):
-            @pl.when((chip - step >= 0) & (chip + 1 < chips))
-            def _():
-                h_right(dp, p, step).wait_send()
-
-            @pl.when((chip + step < chips) & (chip >= 1))
-            def _():
-                h_left(dp, p, step).wait_send()
-
             h_send(dp, p, partner, pair_send.at[PIECES * step + p]).wait_send()
 
 
@@ -464,14 +503,16 @@
     tokens, width = d_out.shape
     slot_rows = slots // n_sp
     block = width // n_dp
-    tn, th = width // 8, min(256, hid_width)
+    tn, th = width // 8, min(256, hid_width // 8)
     n_col = width // tn
     chips = n_dp // 2
+    late = slots - CUTS[-1 - LATE] * slots // CUTS[-1]
     f32, bf = jnp.float32, jnp.bfloat16
     dma = pltpu.SemaphoreType.DMA
     hbm = pl.BlockSpec(memory_space=pl.ANY)
     vmem = pl.BlockSpec(memory_space=pltpu.VMEM)
     buffers = [
+        (ids.shape, ids.dtype), (logits.shape, logits.dtype),
         ((slots, hid_width), bf), ((slots, hid_width), bf), ((tokens, width), bf),
         ((n_dp, slots, hid_width), bf), ((n_dp, n_sp, slot_rows, block), bf),
         ((n_sp, slot_rows, width), bf), ((n_sp, slot_rows, width), bf), ((n_sp, slot_rows, width), bf),
@@ -481,16 +522,16 @@
     ]
     results = [
         ((tokens, width), bf), ((2, tokens), f32), ((slots, hid_width), bf), ((slots, hid_width), bf),
-        ((hid_width, block), f32),
+        ((hid_width, block), f32), ((2 * late, hid_width), bf), ((2 * late, block), bf),
     ]
     kept = sum(math.prod(shape) * jnp.dtype(dtype).itemsize for shape, dtype in results)
     return pl.pallas_call(
         functools.partial(fused_kernel, n_dp, n_sp),
         out_shape=tuple(pltpu.VMEM(shape, dtype) for shape, dtype in results),
-        in_specs=[vmem, vmem, hbm, hbm, hbm, hbm],
-        out_specs=(vmem,) * 5,
+        in_specs=[hbm] * 6,
+        out_specs=(vmem,) * 7,
         scratch_shapes=[pltpu.VMEM(shape, dtype) for shape, dtype in buffers] + [
-            dma((2 * PIECES + 1,)),
+            dma((2 * PIECES + 3,)),
             dma((4,)),
             dma((1,)),
             dma((PIECES * chips,)),
@@ -515,29 +556,40 @@
     )(ids, logits, gate_pre, up_pre, w_down, d_out)
 
 
-def emit_kernel(*refs):
-    count = len(refs) // 2
-    sems = refs[-1]
-    copies = [pltpu.make_async_copy(refs[i], refs[count + i], sems.at[i]) for i in range(count)]
+def finish_kernel(
+    mixed_ref, slopes_ref, ggrad_ref, ugrad_ref, down_ref, late_hid, late_cot,
+    mixed_out, slopes_out, ggrad_out, ugrad_out, down_out, total, sems,
+):
+    done = [(mixed_ref, mixed_out), (slopes_ref, slopes_out), (ggrad_ref, ggrad_out), (ugrad_ref, ugrad_out)]
+    copies = [pltpu.make_async_copy(src, dst, sems.at[i]) for i, (src, dst) in enumerate(done)]
     for copy in copies:
         copy.start()
+    span = total.shape[0] // CHUNKS
+    for chunk in range(CHUNKS):
+        here = slice(chunk * span, (chunk + 1) * span)
+        total[here] = down_ref[here] + lax.dot_general(
+            late_hid[:, here], late_cot[...], (((0,), (0,)), ((), ())), preferred_element_type=jnp.float32
+        )
+        copies.append(pltpu.make_async_copy(total.at[here], down_out.at[here], sems.at[len(done) + chunk]))
+        copies[-1].start()
     for copy in copies:
         copy.wait()
 
 
-def emit(*arrays):
+def finish(*arrays):
+    down = arrays[4]
     return pl.pallas_call(
-        emit_kernel,
-        out_shape=tuple(jax.ShapeDtypeStruct(array.shape, array.dtype) for array in arrays),
+        finish_kernel,
+        out_shape=tuple(jax.ShapeDtypeStruct(array.shape, array.dtype) for array in arrays[:5]),
         in_specs=[pl.BlockSpec(memory_space=pltpu.VMEM)] * len(arrays),
-        out_specs=(pl.BlockSpec(memory_space=pl.ANY),) * len(arrays),
-        scratch_shapes=[pltpu.SemaphoreType.DMA((len(arrays),))],
-        compiler_params=pltpu.CompilerParams(vmem_limit_bytes=1024 * 1024),
+        out_specs=(pl.BlockSpec(memory_space=pl.ANY),) * 5,
+        scratch_shapes=[pltpu.VMEM(down.shape, down.dtype), pltpu.SemaphoreType.DMA((4 + CHUNKS,))],
+        compiler_params=pltpu.CompilerParams(vmem_limit_bytes=16 * 1024 * 1024),
     )(*[pltpu.with_memory_space_constraint(array, pltpu.VMEM) for array in arrays])
 
 
 def local(n_dp, n_sp, gate_pre, up_pre, w_down, route_logits, expert_ids, d_out):
-    mixed, slopes, gate_grads, up_grads, down_grads = emit(*fused(
+    mixed, slopes, gate_grads, up_grads, down_grads = finish(*fused(
         n_dp, n_sp, expert_ids.T, route_logits.T, gate_pre, up_pre, w_down, d_out
     ))
     return (mixed, slopes.T, gate_grads, up_grads, down_grads)

time: 98.1 us -> 94.9 us (0.967)
  Pallas kernels: 97.1 us -> 93.9 us
    pallas_call x1, Pallas kernels: 93.1 us -> 90 us  [fused(): pl.pallas_call(functools.partial(fused_kernel, n_dp, n_sp), out_shape=tup...]
where the time goes in v3:
time: 94.9 us; the launch traced here: 94.5 us
  Pallas kernels  93.9 us (99%)
    pallas_call x1, Pallas kernels, fused(): pl.pallas_call(functools.partial(fused_kernel, n_dp, n_sp), out_shape=tup...  90 us
    pallas_call x1, Pallas kernels, finish(): pl.pallas_call(finish_kernel, out_shape=tuple((jax.ShapeDtypeStruct(array...  3.89 us

profile of v3, /device:TPU:0, one launch (start us, length us, event | category | flops | bytes accessed | tf_op | source)
XLA Modules:
  0.0 94.5 jit_solution(7380570581490743290)
XLA Ops:
  0.6 90.0 %shard_map.101 = (bf16[128,6144]{1,0:T(8,128)(2,1)S(1)}, f32[2,128]{1,0:T(2,128)S(1)}, bf16[256,2048]{1,0:T(8,128)(2,1)S(1)}, bf16[256,2048]{1,0:T(8,128)(2,1)S(...) custom-call(s32[2,128]{1,0:T(2,128)} %bitcast.3, f32[2,128]{1,0:T(2,128)} %bitcast.4, ...), custom_call_target="tpu_custom_call" | custom-call | tf_op jit(solution)/shard_map/pallas_call | solution.py:528
  90.7 3.9 %shard_map.102 = (bf16[128,6144]{1,0:T(8,128)(2,1)}, f32[2,128]{1,0:T(2,128)}, bf16[256,2048]{1,0:T(8,128)(2,1)}, bf16[256,2048]{1,0:T(8,128)(2,1)}, f32[2048,768]{1,0:T(8,128)}) custom-call(bf16[128,6144]{1,0:T(8,128)(2,1)S(1)} %get-tuple-element.17.mixed_ref, f32[2,128]{1,0:T(2,128)S(1)} %get-tuple-element.18.slopes_ref, ...), custom_call_target="tpu_custom_call" | custom-call | tf_op jit(solution)/shard_map/pallas_call | solution.py:581

commit v4 on v3

--- a/solution.py
+++ b/solution.py
@@ -19,9 +19,9 @@
     n_dp, n_sp, ids_hbm, logit_hbm, gate_hbm, up_hbm, w_ref, dout_hbm,
     mixed_ref, lgrad_ref, ggrad_ref, ugrad_ref, down_ref, late_hid, late_cot,
     ids_ref, logit_ref, gate, up, dout, hall, dall, dcyc, part, rs_ref, wcol, wrow,
-    choose_slot, slot_weight, choose_tok, token_weight, wgrad,
+    choose_slot, slot_weight, choose_tok, token_weight, wgrad, shared,
     load_sem, wsem, local_sem, right_send, left_send, pair_send, hrecv, asend, arecv,
-    gsend, grecv, bsend, brecv, rsend, rrecv, fsend, frecv, mate_send,
+    gsend, grecv, bsend, brecv, rsend, rrecv, fsend, frecv, mate_send, mate_recv,
 ):
     f32, bf = jnp.float32, jnp.bfloat16
     dp, sp = lax.axis_index("dp"), lax.axis_index("sp")
@@ -65,8 +65,11 @@
     gate_load(0).start()
     up_load(0).start()
     barrier = pltpu.get_barrier_semaphore()
-    for off in range(1, n_dp):
-        pl.semaphore_signal(barrier, inc=1, device_id={"dp": lax.rem(dp + off, n_dp)}, device_id_type=MESH)
+    for apart in range(1, chips):
+        pl.semaphore_signal(
+            barrier, inc=1, device_id={"dp": 2 * lax.rem(chip + apart, chips) + core}, device_id_type=MESH
+        )
+    pl.semaphore_signal(barrier, inc=1, device_id={"dp": partner}, device_id_type=MESH)
     for off in range(1, n_sp):
         pl.semaphore_signal(barrier, inc=1, device_id={"sp": lax.rem(sp + off, n_sp)}, device_id_type=MESH)
     ids_load.start()
@@ -131,17 +134,26 @@
 
         h_pair(dp, p).start()
 
-    def a_send(apart, to_core):
-        other = 2 * lax.rem(chip + apart, chips) + to_core
+    def a_send(apart):
+        other = lax.rem(chip + apart, chips)
         return remote(
-            dcyc.at[sp, :, block_cols(other)], dall.at[2 * (chips - apart) + core, sp],
-            asend.at[2 * apart + to_core], arecv.at[2 * (chips - apart) + core], dp=other,
-        )
-
-    away = [(apart, to_core) for apart in range(1, chips) for to_core in range(2)]
+            dcyc.at[sp, :, pl.ds(pl.multiple_of(other * 2 * block, 2 * block), 2 * block)], shared.at[chips - apart],
+            asend.at[apart], arecv.at[chips - apart], dp=2 * other + core,
+        )
+
+    def a_own(rel):
+        return pltpu.make_async_copy(
+            shared.at[rel, :, block_cols(core)], dall.at[2 * rel + core, sp], local_sem.at[rel]
+        )
+
+    def a_mate(rel):
+        return remote(
+            shared.at[rel, :, block_cols(1 - core)], dall.at[2 * rel + core, sp],
+            mate_send.at[rel], mate_recv.at[rel], dp=partner,
+        )
 
     make_hidden(0)
-    pl.semaphore_wait(barrier, n_dp - 1 + n_sp - 1)
+    pl.semaphore_wait(barrier, chips + n_sp - 1)
     send_own(0)
 
     ids_load.wait()
@@ -203,8 +215,8 @@
 
     for way in ways:
         g_send(way).start()
-    for apart, to_core in away:
-        a_send(apart, to_core).start()
+    for apart in range(1, chips):
+        a_send(apart).start()
     for p in range(1, PIECES):
         make_hidden(p)
         send_own(p)
@@ -295,8 +307,13 @@
             h_pair(index, p).start()
 
     last = chips - 1
-    for slot in range(2, n_dp):
-        arrived(dall.at[slot, sp], arecv.at[slot])
+    for rel in range(1, chips):
+        arrived(shared.at[rel], arecv.at[rel])
+        a_own(rel).start()
+        a_mate(rel).start()
+    for rel in range(1, chips):
+        a_own(rel).wait()
+        arrived(dall.at[2 * rel + 1 - core, sp], mate_recv.at[rel])
     for way in ways:
         b_send(way).start()
     for way in ways:
@@ -323,7 +340,7 @@
 
     own_copy = pltpu.make_async_copy(dcyc.at[:, :, block_cols(dp)], dall.at[core], local_sem.at[0])
     mate_copy = remote(
-        dcyc.at[:, :, block_cols(partner)], dall.at[core], mate_send.at[0], arecv.at[core], dp=partner
+        dcyc.at[:, :, block_cols(partner)], dall.at[core], mate_send.at[0], mate_recv.at[0], dp=partner
     )
     own_copy.start()
     mate_copy.start()
@@ -373,7 +390,7 @@
                 down_ref[:, cols] += product
 
     own_copy.wait()
-    arrived(dall.at[1 - core], arecv.at[1 - core])
+    arrived(dall.at[1 - core], mate_recv.at[0])
     for p in range(PIECES):
         h_wait(partner, p)
     down_pass(chip, slots, True)
@@ -458,8 +475,9 @@
         if relayed:
             g_pass(way).wait_send()
             b_pass(way).wait_send()
-    for apart, to_core in away:
-        a_send(apart, to_core).wait_send()
+    for apart in range(1, chips):
+        a_send(apart).wait_send()
+        a_mate(apart).wait_send()
 
     def sent(step, p):
         @pl.when((chip - step >= 0) & (chip + 1 < chips))
@@ -518,7 +536,7 @@
         ((n_sp, slot_rows, width), bf), ((n_sp, slot_rows, width), bf), ((n_sp, slot_rows, width), bf),
         ((2, hid_width, tn), bf), ((2, th, width), bf),
         ((slot_rows, tokens), bf), ((slot_rows, 1), f32), ((tokens, tokens), bf), ((tokens, tokens), f32),
-        ((tokens, 1), f32),
+        ((tokens, 1), f32), ((chips, slot_rows, 2 * block), bf),
     ]
     results = [
         ((tokens, width), bf), ((2, tokens), f32), ((slots, hid_width), bf), ((slots, hid_width), bf),
@@ -533,13 +551,13 @@
         scratch_shapes=[pltpu.VMEM(shape, dtype) for shape, dtype in buffers] + [
             dma((2 * PIECES + 3,)),
             dma((4,)),
-            dma((1,)),
+            dma((chips,)),
             dma((PIECES * chips,)),
             dma((PIECES * chips,)),
             dma((PIECES * chips,)),
             dma((PIECES * n_dp,)),
-            dma((n_dp,)),
-            dma((n_dp,)),
+            dma((chips,)),
+            dma((chips,)),
             dma((n_sp,)),
             dma((n_sp,)),
             dma((n_sp,)),
@@ -548,7 +566,8 @@
             dma((n_col, max(n_sp, 6))),
             dma((4,)),
             dma((4,)),
-            dma((1,)),
+            dma((chips,)),
+            dma((chips,)),
         ],
         compiler_params=pltpu.CompilerParams(
             collective_id=0, has_side_effects=True, vmem_limit_bytes=62 * 1024 * 1024 - kept

time: 94.9 us -> 94.4 us (level)
  no operation moved by 1% of the time
where the time goes in v4:
time: 94.4 us; the launch traced here: 94 us
  Pallas kernels  93.3 us (99%)
    pallas_call x1, Pallas kernels, fused(): pl.pallas_call(functools.partial(fused_kernel, n_dp, n_sp), out_shape=tup...  89.4 us
    pallas_call x1, Pallas kernels, finish(): pl.pallas_call(finish_kernel, out_shape=tuple((jax.ShapeDtypeStruct(array...  3.89 us

profile of v4, /device:TPU:0, one launch (start us, length us, event | category | flops | bytes accessed | tf_op | source)
XLA Modules:
  0.0 94.0 jit_solution(17817327714287921614)
XLA Ops:
  0.6 89.4 %shard_map.101 = (bf16[128,6144]{1,0:T(8,128)(2,1)S(1)}, f32[2,128]{1,0:T(2,128)S(1)}, bf16[256,2048]{1,0:T(8,128)(2,1)S(1)}, bf16[256,2048]{1,0:T(8,128)(2,1)S(...) custom-call(s32[2,128]{1,0:T(2,128)} %bitcast.3, f32[2,128]{1,0:T(2,128)} %bitcast.4, ...), custom_call_target="tpu_custom_call" | custom-call | tf_op jit(solution)/shard_map/pallas_call | solution.py:546
  90.1 3.9 %shard_map.102 = (bf16[128,6144]{1,0:T(8,128)(2,1)}, f32[2,128]{1,0:T(2,128)}, bf16[256,2048]{1,0:T(8,128)(2,1)}, bf16[256,2048]{1,0:T(8,128)(2,1)}, f32[2048,768]{1,0:T(8,128)}) custom-call(bf16[128,6144]{1,0:T(8,128)(2,1)S(1)} %get-tuple-element.17.mixed_ref, f32[2,128]{1,0:T(2,128)S(1)} %get-tuple-element.18.slopes_ref, ...), custom_call_target="tpu_custom_call" | custom-call | tf_op jit(solution)/shard_map/pallas_call | solution.py:600
